TPU v7x, 256 devices: a whole 4x4x8 slice. The times are simulated.
256 devices in a mesh: section: 8 (over y_hi, x), seq: 32 (over z, y_lo, core).
Axes of the slice: x: 4, y: 4 (y_hi: 2, y_lo: 2; y = y_hi * 2 + y_lo), z: 8, core: 2. Of those that a mesh axis runs over, the one named last changes fastest.
Arguments:
- features: bfloat16 [4096, 8192], P('seq', 'section'), may hold values from -600 to 600
- norm_gain: float32 [8192], P('section'), may hold values from 0.1 to 1.9
- kv_weight: bfloat16 [8192, 2048], P('section'), may hold values from -0.09375 to 0.09375
- queries: bfloat16 [3, 64, 4096, 128], P(None, 'section', 'seq'), may hold values from -64 to 64
- step_kv: bfloat16 [3, 8, 4096, 256], P(None, 'section', 'seq'), may hold values from -6 to 6
- doc_ids: int32 [4096], replicated, may hold values from 0 to 7, never falling along the last dimension, each value on 1 to 3072 neighbouring positions
- block_lists: int32 [3, 64, 16], replicated, may hold values from 0 to 63, as said below
Outputs:
- attended: bfloat16 [3, 64, 4096, 128], P(None, 'section', 'seq')
- kv_cache: bfloat16 [8, 4096, 256], P('section', 'seq')
Inputs may be any that keep to these rules, and one draw needn't show every extreme that they name: `doc_ids`: document numbers never fall along the tokens; a document holds 1 to 3072 tokens, and one holds exactly 3072. `block_lists`: entry [k, b, 0] is b itself; every entry of row b is at most b; entries may repeat.
All inputs are finite; a program needn't handle non-finite values.
Results may differ from a plain program's by a relative error of at most 0.0084.
Values may be sent and summed in bfloat16 or wider, within the bound.
No kernel may reach another device: no remote copies, remote signals or barrier semaphores. Data moves between devices by JAX's collectives and lax.ppermute only.
A program may use at most 128 MiB of HBM per device.

v0:
```python
import math

import jax
import jax.numpy as jnp
from jax import lax
from jax.sharding import PartitionSpec as P

neg_fill = -1e30


def row_marks(doc_ids, block_lists, anchor, amount, block_len, blocks):
    positions = anchor + jnp.arange(amount, dtype=jnp.int32)
    row_docs = lax.dynamic_slice_in_dim(doc_ids, anchor, amount, 0)
    row_lists = lax.dynamic_slice_in_dim(block_lists, anchor // block_len, amount // block_len, 1)
    row_table = jnp.any(row_lists[..., None] == jnp.arange(blocks, dtype=jnp.int32), axis=2)
    return (positions, row_docs, jnp.repeat(row_table, block_len, axis=1))


def per_device(features, norm_gain, kv_weight, queries, step_kv, doc_ids, block_lists):
    sections = lax.axis_size("section")
    own_shard = lax.axis_index("seq")
    step_total, local_heads, tok_dev, head_dim = queries.shape
    local_groups = step_kv.shape[1]
    group_size = local_heads // local_groups
    feature_width = features.shape[1] * sections
    blocks = block_lists.shape[1]
    block_len = doc_ids.shape[0] // blocks
    floated = features.astype(jnp.float32)
    squares = lax.psum(jnp.sum(floated * floated, axis=1), "section")
    inverse = lax.rsqrt(squares / feature_width + 1e-05)
    normalized = (floated * inverse[:, None] * norm_gain[None, :]).astype(jnp.bfloat16)
    all_groups = kv_weight.shape[1] // (2 * head_dim)
    weight_heads = kv_weight.reshape(kv_weight.shape[0], all_groups, 2 * head_dim)
    kv_cache = lax.psum_scatter(
        jnp.einsum("td,dgc->gtc", normalized, weight_heads, preferred_element_type=jnp.float32),
        "section",
        scatter_dimension=0,
        tiled=True,
    ).astype(jnp.bfloat16)
    own_first = own_shard * tok_dev
    positions, row_docs, row_table = row_marks(
        doc_ids, block_lists, own_first, tok_dev, block_len, blocks
    )
    row_total = queries.shape[2]
    grouped = queries.reshape(step_total, local_groups, group_size, row_total, head_dim)
    inv_sqrt = 1.0 / math.sqrt(head_dim)
    stat_shape = (step_total, local_groups, group_size, row_total)
    initial = (
        jnp.full(stat_shape, neg_fill, jnp.float32),
        jnp.zeros(stat_shape, jnp.float32),
        jnp.zeros(stat_shape + (head_dim,), jnp.float32),
    )
    incoming = lax.all_gather(kv_cache, "seq", axis=1, tiled=True)
    length = incoming.shape[1]
    key_pos = jnp.arange(length, dtype=jnp.int32)
    listed = row_table
    listed = jnp.repeat(listed, block_len, axis=2)
    allowed = (
        listed
        & (key_pos[None, :] <= positions[:, None])[None]
        & (doc_ids[None, :] == row_docs[:, None])[None]
    )

    def attend(running):
        run_max, run_sum, summed = running
        scores = (
            jnp.einsum(
                "skgrd,knd->skgrn",
                grouped,
                incoming[..., :head_dim],
                preferred_element_type=jnp.float32,
            )
            * inv_sqrt
        )
        visible = allowed[:, None, None]
        new_max = jnp.maximum(run_max, jnp.max(jnp.where(visible, scores, neg_fill), axis=-1))
        weights = jnp.where(visible, jnp.exp(scores - new_max[..., None]), 0.0)
        factor = jnp.exp(run_max - new_max)
        run_sum = jnp.sum(weights, axis=-1)
        summed = jnp.einsum(
            "skgrn,knd->skgrd",
            weights.astype(jnp.bfloat16),
            incoming[..., head_dim:],
            preferred_element_type=jnp.float32,
        )
        return (new_max, run_sum, summed)

    run_max, run_sum, summed = lax.cond(jnp.any(allowed), attend, lambda kept: kept, initial)
    step_index = jnp.arange(step_total, dtype=jnp.int32)
    own_mask = (step_index[None, :] <= step_index[:, None])[:, None, None, None, :]
    own_scores = (
        jnp.einsum(
            "skgrd,mkrd->skgrm",
            grouped,
            step_kv[..., :head_dim],
            preferred_element_type=jnp.float32,
        )
        * inv_sqrt
    )
    final_max = jnp.maximum(run_max, jnp.max(jnp.where(own_mask, own_scores, neg_fill), axis=-1))
    own_weights = jnp.where(own_mask, jnp.exp(own_scores - final_max[..., None]), 0.0)
    factor = jnp.exp(run_max - final_max)
    run_sum = run_sum * factor + jnp.sum(own_weights, axis=-1)
    summed = summed * factor[..., None] + jnp.einsum(
        "skgrm,mkrd->skgrd",
        own_weights.astype(jnp.bfloat16),
        step_kv[..., head_dim:],
        preferred_element_type=jnp.float32,
    )
    result = (
        (summed / run_sum[..., None])
        .astype(jnp.bfloat16)
        .reshape(step_total, local_heads, row_total, head_dim)
    )
    return (result, kv_cache)


def solution(mesh):
    in_specs = (
        P("seq", "section"),
        P("section"),
        P("section", None),
        P(None, "section", "seq", None),
        P(None, "section", "seq", None),
        P(),
        P(),
    )
    out_specs = (P(None, "section", "seq", None), P("section", "seq", None))
    return jax.shard_map(
        per_device, mesh=mesh, in_specs=in_specs, out_specs=out_specs, check_vma=False
    )
```

profile of v0, /device:TPU:1, one launch (start us, length us, event | category | flops | bytes accessed | tf_op | source)
XLA Modules:
  0.0 260.7 jit_solution(5253831094713267739)
XLA Ops:
  7.2 1.1 fusion.32
  8.3 21.4 %psum.7 = f32[128]{0:T(128)S(1)} all-reduce(f32[128]{0:T(128)S(1)} %fusion.32), channel_id=1, replica_groups=mesh['section'=8,'seq'=32] {'section'}, use_global_device_ids=true, to_apply=%region_3.4 | all-reduce | flops 128 | bytes 1024 | tf_op jit(solution)/shard_map/psum | solution.py:29
  29.7 4.1 %fusion.26 = f32[8,128,256]{2,1,0:T(8,128)} fusion(bf16[128,8,8,256]{3,2,1,0:T(8,128)(2,1)} %bitcast.126, bf16[128,1024]{1,0:T(8,128)(2,1)} %param.9, f32[1024]{0:T(1024)} %param.10, f32[128]{0:T(128)S(1)} %add_rsqrt_fusion), kind=kOutput, calls=%fused_computation.31 | convolution fusion | flops 537395200 | bytes 5509632 | tf_op jit(solution)/shard_map/td,dgc->gtc/dot_general | solution.py:35
  33.9 77.5 %reduce-scatter.2.cloned.1.call-done = f32[1,128,256]{2,1,0:T(8,128)} async-done(((f32[8,128,256]{2,1,0:T(8,128)}), f32[1,128,256]{2,1,0:T(8,128)}) %reduce-scatter.2.cloned.1.call-update) | async-done | bytes 131088 | tf_op jit(solution)/shard_map/reduce_scatter | solution.py:34
  111.4 1.5 convert_element_type.24
  113.6 1.4 broadcast_compare_fusion.1
  115.0 2.8 %and_reduce_fusion = pred[]{:T(512)} fusion(pred[128,64,64]{0,2,1:T(8,128)(4,1)S(1)} %get-tuple-element.63, pred[128,64,64]{0,2,1:T(8,128)(4,1)S(1)} %get-tuple-element.64, pred[3,128,64]{1,2,0:T(8,128)(4,1)S(1)} %copy.46), kind=kLoop, calls=%fused_computation.24 | loop fusion | flops 4718591 | bytes 1073153 | tf_op jit(solution)/shard_map/reduce_or | solution.py:88
  118.5 2.8 %select_reduce_fusion = (f32[3,8,128]{1,0,2:T(4,128)S(1)}, f32[3,1,8,128,3]{2,4,0,3,1:T(4,128)S(1)}) fusion(pred[3,3]{1,0:T(4,128)(4,1)S(1)} %iota_compare_fusion.1, bf16[3,8,128,128]{3,2,1,0:T(8,128)(2,1)S(1)} %copy-done.4, bf16[3,1,128,128]{3,2,1,0:T(8,128)(2,1)S(1)} %get-tuple-element.60), kind=kOutput, calls=%fused_computation.39 | convolution fusion | flops 2383872 | bytes 933897 | tf_op jit(solution)/shard_map/skgrd,mkrd->skgrm/dot_general | solution.py:92
  121.3 58.8 %all-gather.2.cloned.1.call-done = bf16[1,4096,256]{2,1,0:T(8,128)(2,1)} async-done(((bf16[1,128,256]{2,1,0:T(8,128)(2,1)}), bf16[1,4096,256]{2,1,0:T(8,128)(2,1)}) %all-gather.2.cloned.1.call-update) | async-done | bytes 2097168 | tf_op jit(solution)/shard_map/all_gather | solution.py:53
  180.1 0.4 broadcast_in_dim.75
  180.6 67.9 %conditional.1 = (f32[3,1,8,128,128]{4,2,0,3,1:T(8,128)}, f32[3,1,8,128]{2,0,3,1:T(4,128)S(1)}, f32[3,1,8,128]{2,0,3,1:T(4,128)S(1)}) conditional(s32[]{:T(128)} %convert_element_type.21, () %tuple.16, (pred[3,128,64,64]{1,3,2,0:T(8,128)(4,1)S(1)}, s32[128]{0:T(128)S(1)}, s32[1,128,4096]{1,2,0:T(8,128)S(1)}, s32[4096]{0:T(1024)S(1)}, ...), branch_computations={%region_5.6_spmd, %region_6.9_spmd} | conditional | flops 6585054208 | bytes 173954112 | solution.py:88
  180.7 0.3 compare_bitcast_fusion
  180.9 0.6 copy-done.5
  181.5 1.8 broadcast_compare_fusion
  183.4 1.3 fusion.9
  184.6 20.8 %fusion = (f32[3,8,128]{2,1,0:T(8,128)S(1)}, f32[4096,3,8,128]{3,0,2,1:T(8,128)}) fusion(pred[3,128,4096]{1,2,0:T(8,128)(4,1)S(1)} %fusion.9, bf16[3,8,128,128]{3,2,1,0:T(8,128)(2,1)} %copy-done.5, bf16[1,4096,256]{2,1,0:T(8,128)(2,1)} %get-tuple-element.32), kind=kOutput, calls=%fused_computation.2 | convolution fusion | flops 3258971136 | bytes 53751808 | tf_op jit(solution)/shard_map/cond/branch_1_fun/skgrd,knd->skgrn/dot_general | solution.py:67
  205.5 19.7 %fusion.10 = f32[3,1,8,128,128]{4,3,2,0,1:T(8,128)S(1)} fusion(f32[4096,3,8,128]{3,0,2,1:T(8,128)} %get-tuple-element.56, f32[3,8,128]{2,1,0:T(8,128)S(1)} %get-tuple-element.54, pred[3,128,4096]{1,2,0:T(8,128)(4,1)S(1)} %fusion.9, bf16[1,4096,256]{2,1,0:T(8,128)(2,1)} %get-tuple-element.32), kind=kOutput, calls=%fused_computation.13 | convolution fusion | flops 3271557120 | bytes 54538240 | tf_op jit(solution)/shard_map/cond/branch_1_fun/skgrn,knd->skgrd/dot_general | solution.py:80
  225.2 20.7 %fusion.4 = f32[3,8,128]{2,1,0:T(8,128)S(1)} fusion(f32[4096,3,8,128]{3,0,2,1:T(8,128)} %get-tuple-element.56, f32[3,8,128]{2,1,0:T(8,128)S(1)} %get-tuple-element.54, pred[3,128,4096]{1,2,0:T(8,128)(4,1)S(1)} %fusion.9), kind=kLoop, calls=%fused_computation.6 | loop fusion | flops 50328576 | bytes 51929088 | tf_op jit(solution)/shard_map/cond/branch_1_fun/reduce_sum | solution.py:79
  245.9 2.1 copy.62
  248.1 0.1 copy.64
  248.6 0.8 fusion.35
  249.4 0.2 fusion.49
  249.6 3.2 %fusion.30 = bf16[3,8,128,128]{3,1,0,2:T(8,128)(2,1)S(1)} fusion(f32[3,1,8,128,128]{4,2,0,3,1:T(8,128)} %get-tuple-element.50, f32[3,8,128]{1,0,2:T(4,128)S(1)} %get-tuple-element.58, f32[3,8,128]{1,0,2:T(4,128)S(1)} %get-tuple-element.57, f32[3,1,8,128,3]{2,4,0,3,1:T(4,128)S(1)} %get-tuple-element.62, f32[3,8,128]{1,0,2:T(4,128)S(1)} %fusion.47, ...), kind=kOutput, calls=%fused_computation.34 | convolution fusion | flops 3959808 | bytes 2531337 | tf_op jit(solution)/shard_map/skgrm,mkrd->skgrd/dot_general | solution.py:104
  252.8 1.0 copy.55
  (31 shorter events, 1.1 us)
Async XLA Ops:
  7.2 106.0 %copy-start = (s32[3,64,16]{1,2,0:T(8,128)S(1)}, s32[3,64,16]{1,2,0:T(8,128)}, u32[]{:S(2)}) copy-start(s32[3,64,16]{1,2,0:T(8,128)} %param.15) | copy-start | bytes 36868
  7.2 104.2 %reduce-scatter.2.cloned.1.call-start = ((), (), s32[]{:S(2)}) async-start(), calls=%async_computation.1 | async-start | bytes 1179648 | tf_op jit(solution)/shard_map/reduce_scatter | solution.py:34
  29.7 83.3 %copy-start.3 = (s32[4096]{0:T(1024)S(1)}, s32[4096]{0:T(1024)}, u32[]{:S(2)}) copy-start(s32[4096]{0:T(1024)} %param.14) | copy-start | bytes 49156
  33.8 84.7 %copy-start.2 = (bf16[3,1,128,256]{3,2,1,0:T(8,128)(2,1)S(1)}, bf16[3,1,128,256]{3,2,1,0:T(8,128)(2,1)}, u32[]{:S(2)}) copy-start(bf16[3,1,128,256]{3,2,1,0:T(8,128)(2,1)} %param.13) | copy-start | bytes 589828
  33.8 84.7 %copy-start.4 = (bf16[3,8,128,128]{3,2,1,0:T(8,128)(2,1)S(1)}, bf16[3,8,128,128]{3,2,1,0:T(8,128)(2,1)}, u32[]{:S(2)}) copy-start(bf16[3,8,128,128]{3,2,1,0:T(8,128)(2,1)} %param.12) | copy-start | bytes 2359300
  33.8 146.2 %all-gather.2.cloned.1.call-start = ((), (), s32[]{:S(2)}) async-start(), calls=%async_computation.2 | async-start | bytes 2162688 | tf_op jit(solution)/shard_map/all_gather | solution.py:53
  180.6 0.9 copy-start.5
  249.6 4.3 %copy-start.1 = (s32[3,64,16]{1,2,0:T(8,128)S(1)}, s32[3,64,16]{1,2,0:T(8,128)}, u32[]{:S(2)}) copy-start(s32[3,64,16]{1,2,0:T(8,128)} %param.15) | copy-start | bytes 36868
Sparse Core Ops, SparseCore 0:
  34.0 77.3 reduce-scatter.1
  114.0 66.0 all-gather.1
where the time goes:
time: 261 us
  waiting for transfers between devices  136 us (52%)
  matrix products  50.6 us (19%)
  other arithmetic  32.1 us (12%)
  blocking collectives  21.4 us (8%)
  between operations  14.8 us (6%)
  local copies, waits for them, and re-layouts  5.06 us (2%)
    reduce_scatter x1, waiting for transfers between devices, per_device(): lax.psum_scatter(jnp.einsum('td,dgc->gtc', normalized, weight_heads, pref...  77.5 us
    all_gather x1, waiting for transfers between devices, per_device(): incoming = lax.all_gather(kv_cache, 'seq', axis=1, tiled=True)  58.8 us
    psum x1, blocking collectives, per_device(): squares = lax.psum(jnp.sum(floated * floated, axis=1), 'section')  21.4 us
    dot_general x1, matrix products, attend(): jnp.einsum('skgrd,knd->skgrn', grouped, incoming[..., :head_dim], preferr...  20.8 us
    reduce_sum x1, other arithmetic, attend(): run_sum = jnp.sum(weights, axis=-1)  20.7 us
    dot_general x1, matrix products, attend(): jnp.einsum('skgrn,knd->skgrd', weights.astype(jnp.bfloat16), incoming[......  19.7 us
  transfers between devices with their start and end apart: 2, of which 2 were waited for; matrix products, arithmetic and copies ran while one was open for 3% of the time, Pallas kernels for 0%

commit v1 on v0

v1 whole, which is shorter than its diff:
```python
import functools
import math

import jax
import jax.numpy as jnp
from jax import lax
from jax.experimental import pallas as pl
from jax.experimental.pallas import tpu as pltpu
from jax.sharding import PartitionSpec as P

HEAD = 128
BLK = 64
LIST = 16
DOCS = 8
HIDDEN = -1e30
FAR = 1 << 24
EXTRA = 8
PAIR = 256
SLOTS = 7
LINE = 128
SIZES = (8, 12, 16)

VMEM_ALL = 60 << 20


def project_kernel(feat, gain, weight, out, scaled, tail):
    tokens = feat.shape[0]

    @pl.when(pl.program_id(0) == 0)
    def _():
        x = feat[...].astype(jnp.float32)
        g = x * gain[...]
        high = g.astype(jnp.bfloat16)
        scaled[:tokens] = high
        scaled[tokens:] = (g - high.astype(jnp.float32)).astype(jnp.bfloat16)
        total = jnp.sum(x * x, axis=1, keepdims=True)
        row = jnp.broadcast_to(total, (tokens, 128)).T[:EXTRA]
        top = row.astype(jnp.bfloat16).astype(jnp.float32)
        which = lax.broadcasted_iota(jnp.int32, (EXTRA, 128), 0)
        tail[...] = jnp.where(which == 0, top, jnp.where(which == 1, row - top, 0.0)).astype(jnp.bfloat16)

    product = jnp.dot(scaled[...], weight[...], preferred_element_type=jnp.float32)
    product = (product[:tokens] + product[tokens:]).astype(jnp.bfloat16)
    cols = out.shape[2]
    for j in range(out.shape[0]):
        out[j, :tokens, :] = product[:, j * cols : (j + 1) * cols]
        out[j, tokens:, :128] = tail[...]
        out[j, tokens:, 128:] = jnp.zeros_like(tail)


def project(features, norm_gain, kv_weight, heads):
    tokens, width = features.shape
    cols = kv_weight.shape[1] // heads
    grid = 2
    return pl.pallas_call(
        project_kernel,
        grid=(grid,),
        in_specs=[
            pl.BlockSpec((tokens, width), lambda i: (0, 0)),
            pl.BlockSpec((1, width), lambda i: (0, 0)),
            pl.BlockSpec((width, kv_weight.shape[1] // grid), lambda i: (0, i)),
        ],
        out_specs=pl.BlockSpec((heads // grid, tokens + EXTRA, cols), lambda i: (i, 0, 0)),
        out_shape=jax.ShapeDtypeStruct((heads, tokens + EXTRA, cols), jnp.bfloat16),
        scratch_shapes=[
            pltpu.VMEM((2 * tokens, width), jnp.bfloat16),
            pltpu.VMEM((EXTRA, 128), jnp.bfloat16),
        ],
        compiler_params=pltpu.CompilerParams(vmem_limit_bytes=VMEM_ALL),
        name="project",
    )(features, norm_gain.reshape(1, width), kv_weight)


def reduce_kernel(width, parts, out):
    tokens = out.shape[0]
    total = jnp.sum(parts[:, tokens:, :128].astype(jnp.float32), axis=0)
    squares = jnp.broadcast_to(total[0:1] + total[1:2], (128, tokens)).T
    inverse = lax.rsqrt(squares / width + 1e-05)
    for half in range(2):
        cols = slice(half * 128, half * 128 + 128)
        kept = parts[0, :tokens, cols].astype(jnp.float32)
        for s in range(1, parts.shape[0]):
            kept = kept + parts[s, :tokens, cols].astype(jnp.float32)
        out[:, cols] = (kept * inverse).astype(jnp.bfloat16)


def prepare_kernel(blocks_dev, place, lists, docs, table, seen):
    t = place[0]
    z = t // 4
    low = lax.rem(t, 4)
    units = lists.shape[0]
    d = docs[...]
    starts = [0] + [jnp.sum((d < doc).astype(jnp.int32)) for doc in range(1, DOCS)]
    for doc in range(DOCS):
        table[units * LINE + doc] = starts[doc]
    for c in range(seen.shape[0]):
        seen[c] = -1

    def unit_lists(u, carry):
        block = t * blocks_dev + lax.rem(u, blocks_dev)
        first = block * BLK
        begin = 0
        for doc in range(1, DOCS):
            begin = jnp.where(starts[doc] <= first, starts[doc], begin)
        least = begin // BLK
        for e in range(LIST):
            table[u * LINE + e] = 0
            table[u * LINE + 32 + e] = FAR
        n = 0
        for e in range(LIST):
            c = lists[u, e]
            keep = (c >= least) & (seen[c] != u)
            seen[c] = u
            away = lax.rem(c // 8 - z + 8, 8)
            slot = 0
            for a, s in ((7, 1), (6, 2), (2, 3), (5, 4), (3, 5), (4, 6)):
                slot = jnp.where(away == a, s, slot)
            x = lax.rem(c // 2, 4) ^ low
            row = ((x & 1) * SLOTS + slot) * PAIR + (x >> 1) * (2 * BLK) + lax.rem(c, 2) * BLK
            table[u * LINE + n] = row
            table[u * LINE + 32 + n] = jnp.where(keep, c * BLK, FAR)
            n = n + keep.astype(jnp.int32)
        table[u * LINE + 64] = n
        return carry

    lax.fori_loop(0, units, unit_lists, 0)


def attend_unit(blocks, u, k, half, block, begins, table, queries, own, held):
    last = (((1,), (1,)), ((), ()))
    first = (((0,), (0,)), ((), ()))
    scale = math.log2(math.e) / math.sqrt(HEAD)
    steps = own.shape[0]
    mine = pl.ds(pl.multiple_of(half * BLK, BLK), BLK)
    pieces = [held[pl.ds(pl.multiple_of(table[u * LINE + e], BLK), BLK), :] for e in range(blocks)]
    pieces += [own[m, 0, mine, :] for m in range(steps)]
    kv = jnp.concatenate(pieces, axis=0)
    lane = lax.rem(lax.broadcasted_iota(jnp.int32, (1, 128), 1), BLK)
    sub = lax.broadcasted_iota(jnp.int32, (BLK, 128), 0)
    pos_i = block * BLK + lane
    masks = []
    for e in range(blocks):
        pos_j = table[u * LINE + 32 + e] + sub
        masks.append((pos_j >= begins) & (pos_j <= pos_i))
    for m in range(steps):
        masks.append((sub == lane) & (m <= k))
    mask = jnp.concatenate(masks, axis=0)
    mask = jnp.concatenate([mask] * (queries.shape[0] // 128), axis=1)
    s = lax.dot_general(kv[:, :HEAD], queries, last, preferred_element_type=jnp.float32)
    s = jnp.where(mask, s, HIDDEN)
    top = jnp.max(s, axis=0, keepdims=True)
    p = jnp.exp2((s - top) * scale)
    total = jnp.sum(p, axis=0, keepdims=True)
    summed = lax.dot_general(kv[:, HEAD:], p.astype(jnp.bfloat16), first, preferred_element_type=jnp.float32)
    return (summed / total).T.astype(jnp.bfloat16)


def attend_kernel(blocks_dev, count, place, table, q, own, *refs):
    parts, (out, held, result, sems) = refs[:count], refs[count:]
    t = place[0]
    steps, heads, tokens, head_dim = q.shape
    units = steps * blocks_dev
    row = 0
    for part in parts:
        held[row : row + part.shape[0]] = part[...]
        row += part.shape[0]

    def copy(u):
        rows = pl.ds(pl.multiple_of(lax.rem(u, blocks_dev) * BLK, BLK), BLK)
        return pltpu.make_async_copy(result.at[u], out.at[u // blocks_dev, :, rows, :], sems.at[u])

    def unit_body(u, carry):
        k = u // blocks_dev
        half = lax.rem(u, blocks_dev)
        block = t * blocks_dev + half
        queries = q[k, :, pl.ds(pl.multiple_of(half * BLK, BLK), BLK), :].reshape(heads * BLK, head_dim)
        pos_i = block * BLK + lax.rem(lax.broadcasted_iota(jnp.int32, (1, 128), 1), BLK)
        begins = jnp.zeros((1, 128), jnp.int32)
        for doc in range(1, DOCS):
            start = table[units * LINE + doc]
            begins = jnp.where(start <= pos_i, start, begins)
        n = table[u * LINE + 64]
        least = 0
        for size in SIZES:

            @pl.when((n > least) & (n <= size))
            def _(size=size):
                value = attend_unit(size, u, k, half, block, begins, table, queries, own, held)
                result[u] = value.reshape(heads, BLK, head_dim)

            least = size
        copy(u).start()
        return carry

    lax.fori_loop(0, units, unit_body, 0)
    lax.fori_loop(0, units, lambda u, c: (copy(u).wait(), c)[1], 0)


def attend(place, table, queries, step_kv, parts, blocks_dev):
    steps, heads, tokens, head_dim = queries.shape
    units = steps * blocks_dev
    smem = pl.BlockSpec(memory_space=pltpu.SMEM)
    vmem = pl.BlockSpec(memory_space=pltpu.VMEM)
    return pl.pallas_call(
        functools.partial(attend_kernel, blocks_dev, len(parts)),
        in_specs=[smem, smem, vmem, vmem] + [vmem] * len(parts),
        out_specs=pl.BlockSpec(memory_space=pl.ANY),
        out_shape=jax.ShapeDtypeStruct(queries.shape, jnp.bfloat16),
        scratch_shapes=[
            pltpu.VMEM((2 * SLOTS * PAIR, 2 * head_dim), jnp.bfloat16),
            pltpu.VMEM((units, heads, BLK, head_dim), jnp.bfloat16),
            pltpu.SemaphoreType.DMA((units,)),
        ],
        compiler_params=pltpu.CompilerParams(vmem_limit_bytes=30 << 20),
        name="attend",
    )(place, table, queries, step_kv, *parts)


def per_device(features, norm_gain, kv_weight, queries, step_kv, doc_ids, block_lists):
    sections = lax.axis_size("section")
    seqs = lax.axis_size("seq")
    levels = seqs // 4
    step_total, local_heads, tok_dev, head_dim = queries.shape
    blocks_dev = tok_dev // BLK
    units = step_total * blocks_dev
    place = lax.axis_index("seq").reshape(1).astype(jnp.int32)

    partial = project(features, norm_gain, kv_weight, sections)
    parts = lax.all_to_all(partial, "section", 0, 0, tiled=True)
    kv = pl.pallas_call(
        functools.partial(reduce_kernel, float(features.shape[1] * sections)),
        out_shape=jax.ShapeDtypeStruct((tok_dev, 2 * head_dim), jnp.bfloat16),
        name="reduce",
    )(parts)

    lists = lax.dynamic_slice_in_dim(block_lists, place[0] * blocks_dev, blocks_dev, 1).reshape(units, LIST)
    table = pl.pallas_call(
        functools.partial(prepare_kernel, blocks_dev),
        in_specs=[pl.BlockSpec(memory_space=pltpu.SMEM)] * 2 + [pl.BlockSpec(memory_space=pltpu.VMEM)],
        out_specs=pl.BlockSpec(memory_space=pltpu.SMEM),
        out_shape=jax.ShapeDtypeStruct(((units + 1) * LINE,), jnp.int32),
        scratch_shapes=[pltpu.SMEM((block_lists.shape[1],), jnp.int32)],
        name="prepare",
    )(place, lists, doc_ids.reshape(-1, 128))

    every = range(seqs)
    swap = [(i, i ^ 1) for i in every]
    pair = jnp.concatenate([kv, lax.ppermute(kv, "seq", [(i, i ^ 2) for i in every])], axis=0)
    pair_theirs = lax.ppermute(pair, "seq", swap)
    up = down = pair
    ups, downs = [], []
    for d in range(1, 5):
        pairs = [(i, i + 4) for i in every if i // 4 + 1 < levels and i // 4 - d + 1 >= 0]
        up = lax.ppermute(up, "seq", pairs)
        ups.append(up)
        if d < 4:
            pairs = []
            for i in every:
                origin, goal = (i // 4 + d - 1) % levels, (i // 4 - 1) % levels
                if origin <= 2 and (goal < origin or goal >= 5):
                    pairs.append((i, (i - 4) % seqs))
            down = lax.ppermute(down, "seq", pairs)
            if d == 1:
                up, down, table, pair_theirs = lax.optimization_barrier((up, down, table, pair_theirs))
                ups[0] = up
            downs.append(down)
    near = jnp.concatenate([ups[0], ups[1], downs[1]], axis=0)
    far = jnp.concatenate([ups[2], downs[2]], axis=0)
    mine = [pair, near, far, ups[3]]
    theirs = [pair_theirs] + [lax.ppermute(a, "seq", swap) for a in mine[1:]]
    attended = attend(place, table, queries, step_kv, mine + theirs, blocks_dev)
    return attended, kv[None]


def solution(mesh):
    in_specs = (
        P("seq", "section"),
        P("section"),
        P("section", None),
        P(None, "section", "seq", None),
        P(None, "section", "seq", None),
        P(),
        P(),
    )
    out_specs = (P(None, "section", "seq", None), P("section", "seq", None))
    return jax.shard_map(per_device, mesh=mesh, in_specs=in_specs, out_specs=out_specs, check_vma=False)
```

time: 261 us -> 76.8 us (0.29)
  the two profiles are of different devices: /device:TPU:1 before, /device:TPU:129 now
where the time goes in v1:
time: 76.8 us; the launch traced here: 77.1 us
  starting transfers between devices  22.9 us (30%)
  Pallas kernels  18.5 us (24%)
  blocking collectives  17.7 us (23%)
  waiting for transfers between devices  14.8 us (19%)
  local copies, waits for them, and re-layouts  1.52 us (2%)
  other arithmetic  0.85 us (1%)
  between operations  0.83 us (1%)
    all_to_all x1, blocking collectives, per_device(): parts = lax.all_to_all(partial, 'section', 0, 0, tiled=True)  17.7 us
    ppermute x4, waiting for transfers between devices, per_device(): up = lax.ppermute(up, 'seq', pairs)  10.9 us
    pallas_call x1, Pallas kernels, attend(): pl.pallas_call(functools.partial(attend_kernel, blocks_dev, len(parts)),...  8.94 us
    ppermute x3, starting transfers between devices, per_device(): theirs = [pair_theirs] + [lax.ppermute(a, 'seq', swap) for a in mine[1:]]  8.71 us
    ppermute x4, starting transfers between devices, per_device(): up = lax.ppermute(up, 'seq', pairs)  8.39 us
    pallas_call x1, Pallas kernels, project(): pl.pallas_call(project_kernel, grid=(grid,), in_specs=[pl.BlockSpec((toke...  4.1 us
    pallas_call x1, Pallas kernels, per_device(): pl.pallas_call(functools.partial(prepare_kernel, blocks_dev), in_specs=[p...  3.71 us
    ppermute x1, starting transfers between devices, per_device(): pair_theirs = lax.ppermute(pair, 'seq', swap)  3.38 us
  transfers between devices with their start and end apart: 12, of which 6 were waited for; matrix products, arithmetic and copies ran while one was open for 1% of the time, Pallas kernels for 5%

profile of v1, /device:TPU:129, one launch (start us, length us, event | category | flops | bytes accessed | tf_op | source)
XLA Modules:
  0.0 77.1 jit_solution(13499097073697085865)
XLA Ops:
  0.7 4.1 %project.1 = bf16[8,136,256]{2,1,0:T(8,128)(2,1)} custom-call(bf16[128,1024]{1,0:T(8,128)(2,1)} %feat.1, f32[1,1024]{1,0:T(1,128)} %bitcast.6, bf16[1024,2048]{1,0:T(8,128)(2,1)} %weight.1), custom_call_target="tpu_custom_call" | custom-call | tf_op jit(solution)/shard_map/project/pallas_call | solution.py:55
  4.8 17.7 %all_to_all.5.parts = bf16[8,136,256]{2,1,0:T(8,128)(2,1)} all-to-all(bf16[8,136,256]{2,1,0:T(8,128)(2,1)} %project.1), channel_id=1, replica_groups=mesh['section'=8,'seq'=32] {'section'}, dimensions={0} | all-to-all | bytes 1114112 | tf_op jit(solution)/shard_map/all_to_all | solution.py:229
  22.5 1.8 %reduce.1 = bf16[128,256]{1,0:T(8,128)(2,1)} custom-call(bf16[8,136,256]{2,1,0:T(8,128)(2,1)} %all_to_all.5.parts), custom_call_target="tpu_custom_call" | custom-call | tf_op jit(solution)/shard_map/reduce/pallas_call | solution.py:230
  24.7 2.9 %collective-permute-done = bf16[128,256]{1,0:T(8,128)(2,1)S(1)} collective-permute-done((bf16[128,256]{1,0:T(8,128)(2,1)}, bf16[128,256]{1,0:T(8,128)(2,1)S(1)}, u32[]{:S(2)}, u32[]{:S(2)}) %collective-permute-start) | collective-permute-done | bytes 65568 | tf_op jit(solution)/shard_map/ppermute | solution.py:248
  27.6 0.8 %pad_maximum_fusion.refs_0_ = bf16[256,256]{1,0:T(8,128)(2,1)S(1)} fusion(bf16[128,256]{1,0:T(8,128)(2,1)S(1)} %collective-permute-done, bf16[128,256]{1,0:T(8,128)(2,1)} %reduce.1), kind=kLoop, calls=%fused_computation | loop fusion | flops 262144 | bytes 262144 | tf_op jit(solution)/shard_map/concatenate | solution.py:248
  28.4 3.4 %collective-permute-start.3 = (bf16[256,256]{1,0:T(8,128)(2,1)S(1)}, bf16[256,256]{1,0:T(8,128)(2,1)S(1)}, u32[]{:S(2)}, u32[]{:S(2)}) collective-permute-start(bf16[256,256]{1,0:T(8,128)(2,1)S(1)} %pad_maximum_fusion.refs_0_), channel_id=1, source_target_pairs={{0,1},{1,0},{2,3},{3,2},{4,5},{5,4},{6,7},{7,6},{8,9},{9,8},{10,11... | collective-permute-start | bytes 393224 | tf_op jit(solution)/shard_map/ppermute | solution.py:249
  31.8 0.7 collective-permute-start.2
  32.5 2.6 %collective-permute-start.1 = (bf16[256,256]{1,0:T(8,128)(2,1)S(1)}, bf16[256,256]{1,0:T(8,128)(2,1)S(1)}, u32[]{:S(2)}, u32[]{:S(2)}) collective-permute-start(bf16[256,256]{1,0:T(8,128)(2,1)S(1)} %pad_maximum_fusion.refs_0_), channel_id=1, source_target_pairs={{0,4},{1,5},{2,6},{3,7},{4,8},{5,9},{6,10},{7,11},{8,12},{9,13},{1... | collective-permute-start | bytes 393224 | tf_op jit(solution)/shard_map/ppermute | solution.py:254
  35.9 3.7 %prepare.1.table = s32[896]{0:T(1024)} custom-call(s32[1]{0:T(128)} %bitcast.place, s32[6,16]{1,0:T(8,128)} %reshape.18.lists, s32[32,128]{1,0:T(8,128)} %bitcast.5), custom_call_target="tpu_custom_call" | custom-call | tf_op jit(solution)/shard_map/prepare/pallas_call | solution.py:237
  39.7 1.0 %collective-permute-done.1 = bf16[256,256]{1,0:T(8,128)(2,1)S(1)} collective-permute-done((bf16[256,256]{1,0:T(8,128)(2,1)S(1)}, bf16[256,256]{1,0:T(8,128)(2,1)S(1)}, u32[]{:S(2)}, u32[]{:S(2)}) %collective-permute-start.1) | collective-permute-done | bytes 131104 | tf_op jit(solution)/shard_map/ppermute | solution.py:254
  40.7 0.7 collective-permute-start.5
  41.4 1.9 %collective-permute-start.4 = (bf16[256,256]{1,0:T(8,128)(2,1)S(1)}, bf16[256,256]{1,0:T(8,128)(2,1)S(1)}, u32[]{:S(2)}, u32[]{:S(2)}) collective-permute-start(bf16[256,256]{1,0:T(8,128)(2,1)S(1)} %collective-permute-done.1), channel_id=1, source_target_pairs={{4,8},{5,9},{6,10},{7,11},{8,12},{9,13},{10,14},{11,15},{12,16},{1... | collective-permute-start | bytes 393224 | tf_op jit(solution)/shard_map/ppermute | solution.py:254
  43.3 0.7 collective-permute-start.7
  44.0 4.7 %collective-permute-done.4 = bf16[256,256]{1,0:T(8,128)(2,1)S(1)} collective-permute-done((bf16[256,256]{1,0:T(8,128)(2,1)S(1)}, bf16[256,256]{1,0:T(8,128)(2,1)S(1)}, u32[]{:S(2)}, u32[]{:S(2)}) %collective-permute-start.4) | collective-permute-done | bytes 131104 | tf_op jit(solution)/shard_map/ppermute | solution.py:254
  48.7 1.9 %collective-permute-start.6 = (bf16[256,256]{1,0:T(8,128)(2,1)S(1)}, bf16[256,256]{1,0:T(8,128)(2,1)S(1)}, u32[]{:S(2)}, u32[]{:S(2)}) collective-permute-start(bf16[256,256]{1,0:T(8,128)(2,1)S(1)} %collective-permute-done.4), channel_id=1, source_target_pairs={{8,12},{9,13},{10,14},{11,15},{12,16},{13,17},{14,18},{15,19},{16,... | collective-permute-start | bytes 393224 | tf_op jit(solution)/shard_map/ppermute | solution.py:254
  50.6 1.8 %collective-permute-start.9 = (bf16[768,256]{1,0:T(8,128)(2,1)S(1)}, bf16[768,256]{1,0:T(8,128)(2,1)S(1)}, u32[]{:S(2)}, u32[]{:S(2)}) collective-permute-start(bf16[768,256]{1,0:T(8,128)(2,1)S(1)} %constant_dynamic-update-slice_fusion.refs_1_), channel_id=1, source_target_pairs={{0,1},{1,0},{2,3},{3,2},{4,5},{5,4},{6,7},{7,6},{8,9},{9,8},{10,11... | collective-permute-start | bytes 1179656 | tf_op jit(solution)/shard_map/ppermute | solution.py:270
  52.4 3.2 %collective-permute-done.6 = bf16[256,256]{1,0:T(8,128)(2,1)S(1)} collective-permute-done((bf16[256,256]{1,0:T(8,128)(2,1)S(1)}, bf16[256,256]{1,0:T(8,128)(2,1)S(1)}, u32[]{:S(2)}, u32[]{:S(2)}) %collective-permute-start.6) | collective-permute-done | bytes 131104 | tf_op jit(solution)/shard_map/ppermute | solution.py:254
  55.6 1.9 %collective-permute-start.8 = (bf16[256,256]{1,0:T(8,128)(2,1)S(1)}, bf16[256,256]{1,0:T(8,128)(2,1)S(1)}, u32[]{:S(2)}, u32[]{:S(2)}) collective-permute-start(bf16[256,256]{1,0:T(8,128)(2,1)S(1)} %collective-permute-done.6), channel_id=1, source_target_pairs={{12,16},{13,17},{14,18},{15,19},{16,20},{17,21},{18,22},{19,23},{2... | collective-permute-start | bytes 393224 | tf_op jit(solution)/shard_map/ppermute | solution.py:254
  57.6 2.9 %collective-permute-start.10 = (bf16[512,256]{1,0:T(8,128)(2,1)S(1)}, bf16[512,256]{1,0:T(8,128)(2,1)S(1)}, u32[]{:S(2)}, u32[]{:S(2)}) collective-permute-start(bf16[512,256]{1,0:T(8,128)(2,1)S(1)} %constant_dynamic-update-slice_fusion.3.refs_2_), channel_id=1, source_target_pairs={{0,1},{1,0},{2,3},{3,2},{4,5},{5,4},{6,7},{7,6},{8,9},{9,8},{10,11... | collective-permute-start | bytes 786440 | tf_op jit(solution)/shard_map/ppermute | solution.py:270
  60.5 2.0 %collective-permute-done.8.refs_3_ = bf16[256,256]{1,0:T(8,128)(2,1)S(1)} collective-permute-done((bf16[256,256]{1,0:T(8,128)(2,1)S(1)}, bf16[256,256]{1,0:T(8,128)(2,1)S(1)}, u32[]{:S(2)}, u32[]{:S(2)}) %collective-permute-start.8) | collective-permute-done | bytes 131104 | tf_op jit(solution)/shard_map/ppermute | solution.py:254
  62.5 4.0 %collective-permute-start.11 = (bf16[256,256]{1,0:T(8,128)(2,1)S(1)}, bf16[256,256]{1,0:T(8,128)(2,1)S(1)}, u32[]{:S(2)}, u32[]{:S(2)}) collective-permute-start(bf16[256,256]{1,0:T(8,128)(2,1)S(1)} %collective-permute-done.8.refs_3_), channel_id=1, source_target_pairs={{0,1},{1,0},{2,3},{3,2},{4,5},{5,4},{6,7},{7,6},{8,9},{9,8},{10,11... | collective-permute-start | bytes 393224 | tf_op jit(solution)/shard_map/ppermute | solution.py:270
  66.5 1.0 %collective-permute-done.11.refs_7_ = bf16[256,256]{1,0:T(8,128)(2,1)S(1)} collective-permute-done((bf16[256,256]{1,0:T(8,128)(2,1)S(1)}, bf16[256,256]{1,0:T(8,128)(2,1)S(1)}, u32[]{:S(2)}, u32[]{:S(2)}) %collective-permute-start.11) | collective-permute-done | bytes 131104 | tf_op jit(solution)/shard_map/ppermute | solution.py:270
  67.5 0.7 copy-done.3
  68.2 8.9 %attend.1 = bf16[3,8,128,128]{3,2,1,0:T(8,128)(2,1)} custom-call(s32[1]{0:T(128)} %bitcast.place, s32[896]{0:T(1024)S(1)} %copy-done.3, bf16[3,8,128,128]{3,2,1,0:T(8,128)(2,1)S(1)} %copy-done.1, bf16[3,1,128,256]{3,2,1,0:T(8,128)(2,1)S(1)} %copy-done.2, bf16[256,256]{1,0:T(8,128)(2,1)S(1)} %pad_maximum_fusion.refs_0_, ...), custom_call_target="tpu_custom_call" | custom-call | tf_op jit(solution)/shard_map/attend/pallas_call | solution.py:204
  (22 shorter events, 1.3 us)
Async XLA Ops:
  0.6 34.5 %copy-start = (s32[3,64,16]{1,2,0:T(8,128)S(1)}, s32[3,64,16]{1,2,0:T(8,128)}, u32[]{:S(2)}) copy-start(s32[3,64,16]{1,2,0:T(8,128)} %param.13) | copy-start | bytes 36868
  0.6 66.9 %copy-start.1 = (bf16[3,8,128,128]{3,2,1,0:T(8,128)(2,1)S(1)}, bf16[3,8,128,128]{3,2,1,0:T(8,128)(2,1)}, u32[]{:S(2)}) copy-start(bf16[3,8,128,128]{3,2,1,0:T(8,128)(2,1)} %q.1) | copy-start | bytes 2359300
  0.7 66.9 %copy-start.2 = (bf16[3,1,128,256]{3,2,1,0:T(8,128)(2,1)S(1)}, bf16[3,1,128,256]{3,2,1,0:T(8,128)(2,1)}, u32[]{:S(2)}) copy-start(bf16[3,1,128,256]{3,2,1,0:T(8,128)(2,1)} %own.1) | copy-start | bytes 589828
  24.3 3.3 %collective-permute-start = (bf16[128,256]{1,0:T(8,128)(2,1)}, bf16[128,256]{1,0:T(8,128)(2,1)S(1)}, u32[]{:S(2)}, u32[]{:S(2)}) collective-permute-start(bf16[128,256]{1,0:T(8,128)(2,1)} %reduce.1), channel_id=1, source_target_pairs={{0,2},{1,3},{2,0},{3,1},{4,6},{5,7},{6,4},{7,5},{8,10},{9,11},{10,... | collective-permute-start | bytes 196616 | tf_op jit(solution)/shard_map/ppermute | solution.py:248
  28.4 11.2 %collective-permute-start.3 = (bf16[256,256]{1,0:T(8,128)(2,1)S(1)}, bf16[256,256]{1,0:T(8,128)(2,1)S(1)}, u32[]{:S(2)}, u32[]{:S(2)}) collective-permute-start(bf16[256,256]{1,0:T(8,128)(2,1)S(1)} %pad_maximum_fusion.refs_0_), channel_id=1, source_target_pairs={{0,1},{1,0},{2,3},{3,2},{4,5},{5,4},{6,7},{7,6},{8,9},{9,8},{10,11... | collective-permute-start | bytes 393224 | tf_op jit(solution)/shard_map/ppermute | solution.py:249
  31.8 7.8 %collective-permute-start.2 = (bf16[256,256]{1,0:T(8,128)(2,1)S(1)}, bf16[256,256]{1,0:T(8,128)(2,1)S(1)}, u32[]{:S(2)}, u32[]{:S(2)}) collective-permute-start(bf16[256,256]{1,0:T(8,128)(2,1)S(1)} %pad_maximum_fusion.refs_0_), channel_id=1, source_target_pairs={{0,28},{1,29},{2,30},{3,31},{4,0},{5,1},{6,2},{7,3},{8,4},{9,5},{1... | collective-permute-start | bytes 393224 | tf_op jit(solution)/shard_map/ppermute | solution.py:262
  32.5 8.2 %collective-permute-start.1 = (bf16[256,256]{1,0:T(8,128)(2,1)S(1)}, bf16[256,256]{1,0:T(8,128)(2,1)S(1)}, u32[]{:S(2)}, u32[]{:S(2)}) collective-permute-start(bf16[256,256]{1,0:T(8,128)(2,1)S(1)} %pad_maximum_fusion.refs_0_), channel_id=1, source_target_pairs={{0,4},{1,5},{2,6},{3,7},{4,8},{5,9},{6,10},{7,11},{8,12},{9,13},{1... | collective-permute-start | bytes 393224 | tf_op jit(solution)/shard_map/ppermute | solution.py:254
  40.7 2.6 %collective-permute-start.5 = (bf16[256,256]{1,0:T(8,128)(2,1)S(1)}, bf16[256,256]{1,0:T(8,128)(2,1)S(1)}, u32[]{:S(2)}, u32[]{:S(2)}) collective-permute-start(bf16[256,256]{1,0:T(8,128)(2,1)S(1)} %collective-permute-done.2), channel_id=1, source_target_pairs={{0,28},{1,29},{2,30},{3,31},{4,0},{5,1},{6,2},{7,3},{28,24},{29,25... | collective-permute-start | bytes 393224 | tf_op jit(solution)/shard_map/ppermute | solution.py:262
  41.4 7.3 %collective-permute-start.4 = (bf16[256,256]{1,0:T(8,128)(2,1)S(1)}, bf16[256,256]{1,0:T(8,128)(2,1)S(1)}, u32[]{:S(2)}, u32[]{:S(2)}) collective-permute-start(bf16[256,256]{1,0:T(8,128)(2,1)S(1)} %collective-permute-done.1), channel_id=1, source_target_pairs={{4,8},{5,9},{6,10},{7,11},{8,12},{9,13},{10,14},{11,15},{12,16},{1... | collective-permute-start | bytes 393224 | tf_op jit(solution)/shard_map/ppermute | solution.py:254
  43.3 14.2 %collective-permute-start.7 = (bf16[256,256]{1,0:T(8,128)(2,1)S(1)}, bf16[256,256]{1,0:T(8,128)(2,1)S(1)}, u32[]{:S(2)}, u32[]{:S(2)}) collective-permute-start(bf16[256,256]{1,0:T(8,128)(2,1)S(1)} %collective-permute-done.5), channel_id=1, source_target_pairs={{0,28},{1,29},{2,30},{3,31},{24,20},{25,21},{26,22},{27,23},{28,24... | collective-permute-start | bytes 393224 | tf_op jit(solution)/shard_map/ppermute | solution.py:262
  48.7 6.9 %collective-permute-start.6 = (bf16[256,256]{1,0:T(8,128)(2,1)S(1)}, bf16[256,256]{1,0:T(8,128)(2,1)S(1)}, u32[]{:S(2)}, u32[]{:S(2)}) collective-permute-start(bf16[256,256]{1,0:T(8,128)(2,1)S(1)} %collective-permute-done.4), channel_id=1, source_target_pairs={{8,12},{9,13},{10,14},{11,15},{12,16},{13,17},{14,18},{15,19},{16,... | collective-permute-start | bytes 393224 | tf_op jit(solution)/shard_map/ppermute | solution.py:254
  50.6 16.9 %collective-permute-start.9 = (bf16[768,256]{1,0:T(8,128)(2,1)S(1)}, bf16[768,256]{1,0:T(8,128)(2,1)S(1)}, u32[]{:S(2)}, u32[]{:S(2)}) collective-permute-start(bf16[768,256]{1,0:T(8,128)(2,1)S(1)} %constant_dynamic-update-slice_fusion.refs_1_), channel_id=1, source_target_pairs={{0,1},{1,0},{2,3},{3,2},{4,5},{5,4},{6,7},{7,6},{8,9},{9,8},{10,11... | collective-permute-start | bytes 1179656 | tf_op jit(solution)/shard_map/ppermute | solution.py:270
  55.6 6.9 %collective-permute-start.8 = (bf16[256,256]{1,0:T(8,128)(2,1)S(1)}, bf16[256,256]{1,0:T(8,128)(2,1)S(1)}, u32[]{:S(2)}, u32[]{:S(2)}) collective-permute-start(bf16[256,256]{1,0:T(8,128)(2,1)S(1)} %collective-permute-done.6), channel_id=1, source_target_pairs={{12,16},{13,17},{14,18},{15,19},{16,20},{17,21},{18,22},{19,23},{2... | collective-permute-start | bytes 393224 | tf_op jit(solution)/shard_map/ppermute | solution.py:254
  57.6 9.9 %collective-permute-start.10 = (bf16[512,256]{1,0:T(8,128)(2,1)S(1)}, bf16[512,256]{1,0:T(8,128)(2,1)S(1)}, u32[]{:S(2)}, u32[]{:S(2)}) collective-permute-start(bf16[512,256]{1,0:T(8,128)(2,1)S(1)} %constant_dynamic-update-slice_fusion.3.refs_2_), channel_id=1, source_target_pairs={{0,1},{1,0},{2,3},{3,2},{4,5},{5,4},{6,7},{7,6},{8,9},{9,8},{10,11... | collective-permute-start | bytes 786440 | tf_op jit(solution)/shard_map/ppermute | solution.py:270
  62.5 5.0 %collective-permute-start.11 = (bf16[256,256]{1,0:T(8,128)(2,1)S(1)}, bf16[256,256]{1,0:T(8,128)(2,1)S(1)}, u32[]{:S(2)}, u32[]{:S(2)}) collective-permute-start(bf16[256,256]{1,0:T(8,128)(2,1)S(1)} %collective-permute-done.8.refs_3_), channel_id=1, source_target_pairs={{0,1},{1,0},{2,3},{3,2},{4,5},{5,4},{6,7},{7,6},{8,9},{9,8},{10,11... | collective-permute-start | bytes 393224 | tf_op jit(solution)/shard_map/ppermute | solution.py:270
  67.5 0.7 copy-start.3
